TPU v7x, 256 devices: a whole 4x4x8 slice. The times are simulated.
256 devices in a mesh: section: 8 (over y, core), dp: 32 (over z, x).
Axes of the slice: x: 4, y: 4, z: 8, core: 2. Of those that a mesh axis runs over, the one named last changes fastest.
Arguments:
- crop_maps: bfloat16 [32, 4, 2, 8, 8, 640], P('dp'), may hold values from -6 to 6
- target_maps: int32 [32, 4, 2, 8, 8], P('dp'), may hold values 0 or 1
- crop_counts: int32 [32, 4], P('dp'), may hold values from 1 to 2, as said below
- depth_kernels: float32 [8, 49, 640], P('section'), may hold values from -0.875 to 0.875
- weight_in: bfloat16 [8, 640, 2560], P('section', 'dp'), may hold values from -0.25 to 0.25
- weight_out: bfloat16 [8, 2560, 640], P('section', 'dp'), may hold values from -0.125 to 0.125
- head_weight: float32 [640], replicated, may hold values from -0.25 to 0.25
Outputs:
- grad_in: float32 [8, 640, 2560], P('section', 'dp')
- grad_out: float32 [8, 2560, 640], P('section', 'dp')
- grad_kernels: float32 [8, 49, 640], P('section')
- grad_head: float32 [640], replicated
- loss_value: float32 [], replicated
Inputs may be any that keep to these rules, and one draw needn't show every extreme that they name: `crop_counts`: every data group has some micro-batch with exactly 2 crops.
All inputs are finite; a program needn't handle non-finite values. No bound on the sum of `target_maps` on one device may be relied on, other than what follows from the above.
Results may differ from a plain program's by a relative error of at most 0.034.
Values may be sent and summed in bfloat16 or wider, within the bound.
No kernel may reach another device: no remote copies, remote signals or barrier semaphores. Data moves between devices by JAX's collectives and lax.ppermute only.
A program may use at most 128 MiB of HBM per device.

v0:
```python
import jax
import jax.numpy as jnp
from jax import lax
from jax.sharding import PartitionSpec as P

EPSILON = 1e-06
SQRT_HALF = 0.7071067811865476
INV_ROOT_TWO_PI = 0.3989422804014327


def from_behind(value, axis, steps):
    count = lax.axis_size(axis)
    first, last = (max(0, -steps), min(count, count - steps))
    return lax.ppermute(value, axis, [(source, source + steps) for source in range(first, last)])


def depthwise(values, kernel):
    side = values.shape[1]
    padded = jnp.pad(values, ((0, 0), (3, 3), (3, 3), (0, 0)))
    result = jnp.zeros_like(values)
    for vertical in range(7):
        for across in range(7):
            result = (
                result
                + padded[:, vertical : vertical + side, across : across + side, :]
                * kernel[vertical * 7 + across]
            )
    return result


def depthwise_back(grads, kernel):
    side = grads.shape[1]
    padded = jnp.pad(grads, ((0, 0), (3, 3), (3, 3), (0, 0)))
    result = jnp.zeros_like(grads)
    for vertical in range(7):
        for across in range(7):
            result = (
                result
                + padded[:, 6 - vertical : 6 - vertical + side, 6 - across : 6 - across + side, :]
                * kernel[vertical * 7 + across]
            )
    return result


def kernel_grad(values, grads):
    side = values.shape[1]
    padded = jnp.pad(values, ((0, 0), (3, 3), (3, 3), (0, 0)))
    taps = []
    for vertical in range(7):
        for across in range(7):
            taps.append(
                jnp.sum(
                    padded[:, vertical : vertical + side, across : across + side, :] * grads,
                    axis=(0, 1, 2),
                )
            )
    return jnp.stack(taps, axis=0)


def block_parts(tiles, kernel, weight_in):
    width = tiles.shape[-1]
    widened = tiles.astype(jnp.float32)
    mixed = depthwise(widened, kernel).reshape(-1, width)
    centred = mixed - jnp.mean(mixed, axis=-1, keepdims=True)
    inverse = lax.rsqrt(jnp.mean(centred * centred, axis=-1, keepdims=True) + EPSILON)
    normed = centred * inverse
    normed_low = normed.astype(jnp.bfloat16)
    hidden = jnp.dot(normed_low, weight_in, preferred_element_type=jnp.float32)
    activated = (hidden * 0.5 * (1.0 + lax.erf(hidden * SQRT_HALF))).astype(jnp.bfloat16)
    return (widened, normed, inverse, normed_low, hidden, activated)


def block_forward(tiles, kernel, weight_in, weight_out):
    width = tiles.shape[-1]
    widened, normed, inverse, normed_low, hidden, activated = block_parts(tiles, kernel, weight_in)
    output = jnp.dot(activated, weight_out, preferred_element_type=jnp.float32)
    return (widened.reshape(-1, width) + output).astype(jnp.bfloat16).reshape(tiles.shape)


def block_backward(tiles, upstream, kernel, weight_in, weight_out):
    width = tiles.shape[-1]
    widened, normed, inverse, normed_low, hidden, activated = block_parts(tiles, kernel, weight_in)
    up_flat = upstream.reshape(-1, width)
    through = lax.dot_general(
        up_flat, weight_out, (((1,), (1,)), ((), ())), preferred_element_type=jnp.float32
    )
    slope = (
        0.5 * (1.0 + lax.erf(hidden * SQRT_HALF))
        + hidden * jnp.exp(-0.5 * hidden * hidden) * INV_ROOT_TWO_PI
    )
    hidden_grad = (through * slope).astype(jnp.bfloat16)
    normed_grad = lax.dot_general(
        hidden_grad, weight_in, (((1,), (1,)), ((), ())), preferred_element_type=jnp.float32
    )
    mixed_grad = inverse * (
        normed_grad
        - jnp.mean(normed_grad, axis=-1, keepdims=True)
        - normed * jnp.mean(normed_grad * normed, axis=-1, keepdims=True)
    )
    mixed_tiles = mixed_grad.reshape(tiles.shape)
    kernel_term = kernel_grad(widened, mixed_tiles)
    tile_grad = (upstream.astype(jnp.float32) + depthwise_back(mixed_tiles, kernel)).astype(
        jnp.bfloat16
    )
    return (tile_grad, kernel_term, normed_low, hidden_grad, activated, up_flat)


def outer_sum(left, right):
    return lax.dot_general(
        left, right, (((0,), (0,)), ((), ())), preferred_element_type=jnp.float32
    )


def head_terms(final, targets, live, head_weight, factor):
    widened = final.astype(jnp.float32)
    logits = jnp.sum(widened * head_weight, axis=-1)
    weight_live = live.astype(jnp.float32)[:, :, None, None]
    truth = targets.astype(jnp.float32)
    loss_term = jnp.sum(weight_live * (jax.nn.softplus(logits) - truth * logits)) * factor
    logit_grad = (jax.nn.sigmoid(logits) - truth) * weight_live * factor
    seeds = (logit_grad[..., None] * head_weight).astype(jnp.bfloat16)
    head_term = jnp.sum(logit_grad[..., None] * widened, axis=(0, 1, 2, 3))
    return (loss_term, seeds, head_term)


def body(crop_maps, target_maps, crop_counts, depth_kernels, weight_in, weight_out, head_weight):
    section_index = lax.axis_index("section")
    section_count = lax.axis_size("section")
    micro_count = crop_maps.shape[1]
    slot_count = crop_maps.shape[2]
    kernel = depth_kernels[0]
    live = jnp.arange(slot_count)[None, :] < crop_counts[0][:, None]
    entering = crop_maps[0] * live[:, :, None, None, None].astype(jnp.bfloat16)
    first_full, second_full = (
        lax.all_gather(weight_in[0], "dp", axis=0, tiled=True),
        lax.all_gather(weight_out[0], "dp", axis=0, tiled=True),
    )
    blank_tile = jnp.zeros(entering.shape[1:], jnp.bfloat16)
    ticks = micro_count + section_count - 1

    def forward_step(moment, carry):
        arrived, saved, final = carry
        micro = moment - section_index
        active = (micro >= 0) & (micro < micro_count)
        place = jnp.clip(micro, 0, micro_count - 1)
        own_tiles = lax.dynamic_index_in_dim(entering, place, 0, keepdims=False)
        current = jnp.where(section_index == 0, own_tiles, arrived)
        result = lax.cond(
            active,
            lambda tiles: block_forward(tiles, kernel, first_full, second_full),
            lambda tiles: jnp.zeros_like(tiles),
            current,
        )
        old_saved = lax.dynamic_index_in_dim(saved, place, 0, keepdims=False)
        saved = lax.dynamic_update_index_in_dim(
            saved, jnp.where(active, current, old_saved), place, 0
        )
        old_final = lax.dynamic_index_in_dim(final, place, 0, keepdims=False)
        final = lax.dynamic_update_index_in_dim(
            final, jnp.where(active, result, old_final), place, 0
        )
        arrived = from_behind(result, "section", 1)
        return (arrived, saved, final)

    _, saved, final = lax.fori_loop(
        0, ticks, forward_step, (blank_tile, jnp.zeros_like(entering), jnp.zeros_like(entering))
    )
    is_last = section_index == section_count - 1
    last_weight = is_last.astype(jnp.float32)
    factor = 1.0 / (micro_count * slot_count)
    loss_term, seeds, head_term = head_terms(final, target_maps[0], live, head_weight, factor)
    head_total, loss_total = lax.psum(
        (head_term * last_weight, loss_term * last_weight), ("section", "dp")
    )
    first_back, second_back = (
        lax.all_gather(weight_in[0], "dp", axis=0, tiled=True),
        lax.all_gather(weight_out[0], "dp", axis=0, tiled=True),
    )
    width = entering.shape[-1]
    expand = first_back.shape[1]
    extra_start = (jnp.zeros((width, expand), jnp.float32), jnp.zeros((expand, width), jnp.float32))

    def backward_step(moment, carry):
        arrived, kernel_acc, extra = carry
        micro = moment - (section_count - 1 - section_index)
        active = (micro >= 0) & (micro < micro_count)
        place = jnp.clip(micro, 0, micro_count - 1)
        own_seed = lax.dynamic_index_in_dim(seeds, place, 0, keepdims=False)
        upstream = jnp.where(is_last, own_seed, arrived)
        stored = lax.dynamic_index_in_dim(saved, place, 0, keepdims=False)

        def run_block(operands):
            grad_tiles, inputs, acc_kernel, acc_extra = operands
            tile_grad, kernel_term, normed_low, hidden_grad, activated, up_flat = block_backward(
                inputs, grad_tiles, kernel, first_back, second_back
            )
            new_extra = (
                acc_extra[0] + outer_sum(normed_low, hidden_grad),
                acc_extra[1] + outer_sum(activated, up_flat),
            )
            return (tile_grad, acc_kernel + kernel_term, new_extra)

        def skip_block(operands):
            return (jnp.zeros_like(operands[0]), operands[2], operands[3])

        tile_grad, kernel_acc, extra = lax.cond(
            active, run_block, skip_block, (upstream, stored, kernel_acc, extra)
        )
        arrived = from_behind(tile_grad, "section", -1)
        return (arrived, kernel_acc, extra)

    _, kernel_acc, extra = lax.fori_loop(
        0, ticks, backward_step, (blank_tile, jnp.zeros(kernel.shape, jnp.float32), extra_start)
    )
    first_part, second_part = (
        lax.psum_scatter(
            extra[0].astype(jnp.bfloat16), "dp", scatter_dimension=0, tiled=True
        ).astype(jnp.float32),
        lax.psum_scatter(
            extra[1].astype(jnp.bfloat16), "dp", scatter_dimension=0, tiled=True
        ).astype(jnp.float32),
    )
    kernel_total = lax.psum(kernel_acc.astype(jnp.bfloat16), "dp").astype(jnp.float32)
    return (first_part[None], second_part[None], kernel_total[None], head_total, loss_total)


def solution(mesh):
    return jax.shard_map(
        body,
        mesh=mesh,
        in_specs=(
            P("dp", None, None, None, None, None),
            P("dp", None, None, None, None),
            P("dp", None),
            P("section", None, None),
            P("section", "dp", None),
            P("section", "dp", None),
            P(),
        ),
        out_specs=(
            P("section", "dp", None),
            P("section", "dp", None),
            P("section", None, None),
            P(),
            P(),
        ),
        check_vma=False,
    )
```

profile of v0, /device:TPU:1, one launch (start us, length us, event | category | flops | bytes accessed | tf_op | source)
XLA Modules:
  0.0 1533.0 jit_solution(5656709828315738469)
XLA Ops:
  13.1 91.3 %all-gather.5.cloned.1.call-done = bf16[1,640,2560]{2,0,1:T(2,128)(2,1)} async-done(((bf16[1,20,2560]{2,0,1:T(2,128)(2,1)}), bf16[1,640,2560]{2,0,1:T(2,128)(2,1)}) %all-gather.5.cloned.1.call-update) | async-done | bytes 3276816 | tf_op jit(solution)/shard_map/all_gather | solution.py:135
  108.0 72.7 %all-gather.7.cloned.1.call-done = bf16[1,2560,640]{2,1,0:T(8,128)(2,1)} async-done(((bf16[1,80,640]{2,1,0:T(8,128)(2,1)}), bf16[1,2560,640]{2,1,0:T(8,128)(2,1)}) %all-gather.7.cloned.1.call-update) | async-done | bytes 3276816 | tf_op jit(solution)/shard_map/all_gather | solution.py:136
  183.2 210.7 %while.40 = (s32[]{:T(128)}, bf16[2,8,8,640]{3,2,1,0:T(8,128)(2,1)}, bf16[4,2,8,8,640]{4,3,2,1,0:T(8,128)(2,1)}, bf16[4,2,8,8,640]{4,3,2,1,0:T(8,128)(2,1)}, s32...) while((s32[]{:T(128)}, ...), condition=%wide.region_5.6_spmd, body=%wide.region_0.5_spmd.sunk | while | flops 849510528 | bytes 13491009 | solution.py:165
  185.9 7.7 collective-permute-start
  195.4 12.2 collective-permute-done
  210.3 14.7 conditional.5
  231.9 14.7 conditional.5
  256.1 14.7 conditional.5
  280.3 14.7 conditional.5
  304.5 19.2 %collective-permute-start = (bf16[2,8,8,640]{3,2,1,0:T(8,128)(2,1)S(1)}, bf16[2,8,8,640]{3,2,1,0:T(8,128)(2,1)}, u32[]{:S(2)}, u32[]{:S(2)}) collective-permute-start(bf16[2,8,8,640]{3,2,1,0:T(8,128)(2,1)S(1)} %get-tuple-element.1153), channel_id=1, source_target_pairs={{0,32},{32,64},{64,96},{96,128},{128,160},{160,192},{192,224},{1,3... | collective-permute-start | bytes 491528 | tf_op jit(solution)/shard_map/while/body/eval_jaxpr/ppermute | solution.py:14
  338.2 12.7 collective-permute-start
  365.5 16.6 %collective-permute-start = (bf16[2,8,8,640]{3,2,1,0:T(8,128)(2,1)S(1)}, bf16[2,8,8,640]{3,2,1,0:T(8,128)(2,1)}, u32[]{:S(2)}, u32[]{:S(2)}) collective-permute-start(bf16[2,8,8,640]{3,2,1,0:T(8,128)(2,1)S(1)} %get-tuple-element.1153), channel_id=1, source_target_pairs={{0,32},{32,64},{64,96},{96,128},{128,160},{160,192},{192,224},{1,3... | collective-permute-start | bytes 491528 | tf_op jit(solution)/shard_map/while/body/eval_jaxpr/ppermute | solution.py:14
  403.2 778.2 %while.41 = (s32[]{:T(128)}, bf16[2,8,8,640]{3,2,1,0:T(8,128)(2,1)}, f32[49,640]{1,0:T(8,128)S(1)}, f32[640,2560]{1,0:T(8,128)}, f32[2560,640]{1,0:T(8,128)}, /*...) while((s32[]{:T(128)}, ...), condition=%wide.region_63.64_spmd.clone, body=%wide.region_7.63_spmd.clone.sunk | while | flops 2131804288 | bytes 130983528 | solution.py:212
  407.5 14.1 collective-permute-done.1
  435.2 17.3 %collective-permute-done.1 = bf16[2,8,8,640]{3,2,1,0:T(8,128)(2,1)} collective-permute-done((bf16[2,8,8,640]{3,2,1,0:T(8,128)(2,1)}, bf16[2,8,8,640]{3,2,1,0:T(8,128)(2,1)}, u32[]{:S(2)}, u32[]{:S(2)}) %collective-permute-start.1) | collective-permute-done | bytes 163872 | tf_op jit(solution)/shard_map/while/body/eval_jaxpr/ppermute | solution.py:14
  466.1 13.4 collective-permute-done.1
  483.8 359.0 %collective-permute-done.1 = bf16[2,8,8,640]{3,2,1,0:T(8,128)(2,1)} collective-permute-done((bf16[2,8,8,640]{3,2,1,0:T(8,128)(2,1)}, bf16[2,8,8,640]{3,2,1,0:T(8,128)(2,1)}, u32[]{:S(2)}, u32[]{:S(2)}) %collective-permute-start.1) | collective-permute-done | bytes 163872 | tf_op jit(solution)/shard_map/while/body/eval_jaxpr/ppermute | solution.py:14
  844.6 60.5 %conditional.6 = (bf16[2,8,8,640]{3,2,1,0:T(8,128)(2,1)}, f32[49,640]{1,0:T(8,128)S(1)}, f32[640,2560]{1,0:T(8,128)}, f32[2560,640]{1,0:T(8,128)}) conditional(s32[]{:T(128)} %convert_element_type.175, (f32[49,640]{1,0:T(8,128)S(1)}, f32[640,2560]{1,0:T(8,128)}, f32[2560,640]{1,0:T(8,128)}) %tuple.251, (pred[]{:T(512)}, s32[]{:T(128)}, ...), branch_computations={%region_8.8_spmd, %region_9.62_spmd} | conditional | flops 2131148928 | bytes 129667864 | solution.py:206
  884.0 8.0 stack.299
  893.8 7.2 convolution_add_fusion.1
  913.7 60.5 %conditional.6 = (bf16[2,8,8,640]{3,2,1,0:T(8,128)(2,1)}, f32[49,640]{1,0:T(8,128)S(1)}, f32[640,2560]{1,0:T(8,128)}, f32[2560,640]{1,0:T(8,128)}) conditional(s32[]{:T(128)} %convert_element_type.175, (f32[49,640]{1,0:T(8,128)S(1)}, f32[640,2560]{1,0:T(8,128)}, f32[2560,640]{1,0:T(8,128)}) %tuple.251, (pred[]{:T(512)}, s32[]{:T(128)}, ...), branch_computations={%region_8.8_spmd, %region_9.62_spmd} | conditional | flops 2131148928 | bytes 129667864 | solution.py:206
  953.1 8.0 stack.299
  982.8 60.5 %conditional.6 = (bf16[2,8,8,640]{3,2,1,0:T(8,128)(2,1)}, f32[49,640]{1,0:T(8,128)S(1)}, f32[640,2560]{1,0:T(8,128)}, f32[2560,640]{1,0:T(8,128)}) conditional(s32[]{:T(128)} %convert_element_type.175, (f32[49,640]{1,0:T(8,128)S(1)}, f32[640,2560]{1,0:T(8,128)}, f32[2560,640]{1,0:T(8,128)}) %tuple.251, (pred[]{:T(512)}, s32[]{:T(128)}, ...), branch_computations={%region_8.8_spmd, %region_9.62_spmd} | conditional | flops 2131148928 | bytes 129667864 | solution.py:206
  1022.2 8.0 stack.299
  1051.9 60.5 %conditional.6 = (bf16[2,8,8,640]{3,2,1,0:T(8,128)(2,1)}, f32[49,640]{1,0:T(8,128)S(1)}, f32[640,2560]{1,0:T(8,128)}, f32[2560,640]{1,0:T(8,128)}) conditional(s32[]{:T(128)} %convert_element_type.175, (f32[49,640]{1,0:T(8,128)S(1)}, f32[640,2560]{1,0:T(8,128)}, f32[2560,640]{1,0:T(8,128)}) %tuple.251, (pred[]{:T(512)}, s32[]{:T(128)}, ...), branch_computations={%region_8.8_spmd, %region_9.62_spmd} | conditional | flops 2131148928 | bytes 129667864 | solution.py:206
  1091.3 8.0 stack.299
  1101.1 7.2 convolution_add_fusion.1
  1121.6 58.4 %collective-permute-start.1 = (bf16[2,8,8,640]{3,2,1,0:T(8,128)(2,1)}, bf16[2,8,8,640]{3,2,1,0:T(8,128)(2,1)}, u32[]{:S(2)}, u32[]{:S(2)}) collective-permute-start(bf16[2,8,8,640]{3,2,1,0:T(8,128)(2,1)} %get-tuple-element.1051), channel_id=1, source_target_pairs={{32,0},{64,32},{96,64},{128,96},{160,128},{192,160},{224,192},{33,... | collective-permute-start | bytes 491528 | tf_op jit(solution)/shard_map/while/body/eval_jaxpr/ppermute | solution.py:14
  1191.4 84.2 %fusion.2 = bf16[24,2560]{1,0:T(8,128)(2,1)} fusion(bf16[640,2560]{1,0:T(8,128)(2,1)S(1)} %convert_element_type.133), kind=kCustom, calls=%all-reduce-scatter | all-reduce-scatter fusion | flops 1966081 | bytes 3400704
  1283.4 9.5 collective-permute-start.7
  1294.3 110.5 %psum.21 = bf16[1,49,640]{2,0,1:T(2,128)(2,1)S(1)} all-reduce(bf16[1,49,640]{2,0,1:T(2,128)(2,1)S(1)} %broadcast_in_dim.64), channel_id=1, replica_groups=mesh['section'=8,'dp'=32] {'dp'}, use_global_device_ids=true, to_apply=%region_66.67 | all-reduce | flops 31360 | bytes 125440 | tf_op jit(solution)/shard_map/psum | solution.py:223
  1406.9 115.7 %all-reduce.5 = (f32[640]{0:T(1024)}, f32[]{:T(128)}) all-reduce(f32[640]{0:T(1024)S(1)} %broadcast_multiply_fusion.4, f32[]{:T(128)S(6)} %mul.2377), channel_id=1, replica_groups=mesh['section'=8,'dp'=32] {'section','dp'}, use_global_device_ids=true, to_apply=%region_68.69 | all-reduce | flops 641 | bytes 5128 | tf_op jit(solution)/shard_map/psum | solution.py:172
  (1168 shorter events, 456.3 us)
Async XLA Ops:
  7.2 97.2 %all-gather.5.cloned.1.call-start = ((), (), s32[]{:S(2)}) async-start(), calls=%async_computation.2 | async-start | bytes 6758400 | tf_op jit(solution)/shard_map/all_gather | solution.py:135
  9.0 171.6 %all-gather.7.cloned.1.call-start = ((), (), s32[]{:S(2)}) async-start(), calls=%async_computation.3 | async-start | bytes 3379200 | tf_op jit(solution)/shard_map/all_gather | solution.py:136
  9.8 1515.1 %reduce-scatter.4.cloned.1.call-start = ((), (), s32[]{:S(2)}) async-start(), calls=%async_computation.1 | async-start | bytes 3379200 | tf_op jit(solution)/shard_map/reduce_scatter | solution.py:219
  183.2 212.0 %copy-start.81 = (s32[1,4,2,8,8]{4,3,2,1,0:T(8,128)S(1)}, s32[1,4,2,8,8]{4,3,2,1,0:T(8,128)}, u32[]{:S(2)}) copy-start(s32[1,4,2,8,8]{4,3,2,1,0:T(8,128)} %param.16) | copy-start | bytes 6148
  185.9 21.6 %collective-permute-start = (bf16[2,8,8,640]{3,2,1,0:T(8,128)(2,1)S(1)}, bf16[2,8,8,640]{3,2,1,0:T(8,128)(2,1)}, u32[]{:S(2)}, u32[]{:S(2)}) collective-permute-start(bf16[2,8,8,640]{3,2,1,0:T(8,128)(2,1)S(1)} %get-tuple-element.1153), channel_id=1, source_target_pairs={{0,32},{32,64},{64,96},{96,128},{128,160},{160,192},{192,224},{1,3... | collective-permute-start | bytes 491528 | tf_op jit(solution)/shard_map/while/body/eval_jaxpr/ppermute | solution.py:14
  225.0 4.2 collective-permute-start
  246.6 6.8 collective-permute-start
  270.8 6.7 collective-permute-start
  295.0 6.7 collective-permute-start
  304.5 21.4 %collective-permute-start = (bf16[2,8,8,640]{3,2,1,0:T(8,128)(2,1)S(1)}, bf16[2,8,8,640]{3,2,1,0:T(8,128)(2,1)}, u32[]{:S(2)}, u32[]{:S(2)}) collective-permute-start(bf16[2,8,8,640]{3,2,1,0:T(8,128)(2,1)S(1)} %get-tuple-element.1153), channel_id=1, source_target_pairs={{0,32},{32,64},{64,96},{96,128},{128,160},{160,192},{192,224},{1,3... | collective-permute-start | bytes 491528 | tf_op jit(solution)/shard_map/while/body/eval_jaxpr/ppermute | solution.py:14
  328.7 6.7 collective-permute-start
  338.2 14.9 collective-permute-start
  355.9 6.7 collective-permute-start
  365.5 18.8 %collective-permute-start = (bf16[2,8,8,640]{3,2,1,0:T(8,128)(2,1)S(1)}, bf16[2,8,8,640]{3,2,1,0:T(8,128)(2,1)}, u32[]{:S(2)}, u32[]{:S(2)}) collective-permute-start(bf16[2,8,8,640]{3,2,1,0:T(8,128)(2,1)S(1)} %get-tuple-element.1153), channel_id=1, source_target_pairs={{0,32},{32,64},{64,96},{96,128},{128,160},{160,192},{192,224},{1,3... | collective-permute-start | bytes 491528 | tf_op jit(solution)/shard_map/while/body/eval_jaxpr/ppermute | solution.py:14
  387.1 6.7 collective-permute-start
  405.6 16.0 %collective-permute-start.1 = (bf16[2,8,8,640]{3,2,1,0:T(8,128)(2,1)}, bf16[2,8,8,640]{3,2,1,0:T(8,128)(2,1)}, u32[]{:S(2)}, u32[]{:S(2)}) collective-permute-start(bf16[2,8,8,640]{3,2,1,0:T(8,128)(2,1)} %get-tuple-element.1051), channel_id=1, source_target_pairs={{32,0},{64,32},{96,64},{128,96},{160,128},{192,160},{224,192},{33,... | collective-permute-start | bytes 491528 | tf_op jit(solution)/shard_map/while/body/eval_jaxpr/ppermute | solution.py:14
  423.9 6.9 collective-permute-start.1
  433.3 19.2 %collective-permute-start.1 = (bf16[2,8,8,640]{3,2,1,0:T(8,128)(2,1)}, bf16[2,8,8,640]{3,2,1,0:T(8,128)(2,1)}, u32[]{:S(2)}, u32[]{:S(2)}) collective-permute-start(bf16[2,8,8,640]{3,2,1,0:T(8,128)(2,1)} %get-tuple-element.1051), channel_id=1, source_target_pairs={{32,0},{64,32},{96,64},{128,96},{160,128},{192,160},{224,192},{33,... | collective-permute-start | bytes 491528 | tf_op jit(solution)/shard_map/while/body/eval_jaxpr/ppermute | solution.py:14
  454.9 6.9 collective-permute-start.1
  464.2 15.3 %collective-permute-start.1 = (bf16[2,8,8,640]{3,2,1,0:T(8,128)(2,1)}, bf16[2,8,8,640]{3,2,1,0:T(8,128)(2,1)}, u32[]{:S(2)}, u32[]{:S(2)}) collective-permute-start(bf16[2,8,8,640]{3,2,1,0:T(8,128)(2,1)} %get-tuple-element.1051), channel_id=1, source_target_pairs={{32,0},{64,32},{96,64},{128,96},{160,128},{192,160},{224,192},{33,... | collective-permute-start | bytes 491528 | tf_op jit(solution)/shard_map/while/body/eval_jaxpr/ppermute | solution.py:14
  481.9 361.0 %collective-permute-start.1 = (bf16[2,8,8,640]{3,2,1,0:T(8,128)(2,1)}, bf16[2,8,8,640]{3,2,1,0:T(8,128)(2,1)}, u32[]{:S(2)}, u32[]{:S(2)}) collective-permute-start(bf16[2,8,8,640]{3,2,1,0:T(8,128)(2,1)} %get-tuple-element.1051), channel_id=1, source_target_pairs={{32,0},{64,32},{96,64},{128,96},{160,128},{192,160},{224,192},{33,... | collective-permute-start | bytes 491528 | tf_op jit(solution)/shard_map/while/body/eval_jaxpr/ppermute | solution.py:14
  905.0 6.9 collective-permute-start.1
  974.1 6.9 collective-permute-start.1
  1043.2 6.9 collective-permute-start.1
  1112.3 6.9 collective-permute-start.1
  1121.6 59.7 %collective-permute-start.1 = (bf16[2,8,8,640]{3,2,1,0:T(8,128)(2,1)}, bf16[2,8,8,640]{3,2,1,0:T(8,128)(2,1)}, u32[]{:S(2)}, u32[]{:S(2)}) collective-permute-start(bf16[2,8,8,640]{3,2,1,0:T(8,128)(2,1)} %get-tuple-element.1051), channel_id=1, source_target_pairs={{32,0},{64,32},{96,64},{128,96},{160,128},{192,160},{224,192},{33,... | collective-permute-start | bytes 491528 | tf_op jit(solution)/shard_map/while/body/eval_jaxpr/ppermute | solution.py:14
  1276.5 246.1 %collective-permute-start.6 = (bf16[24,2560]{1,0:T(8,128)(2,1)}, bf16[24,2560]{1,0:T(8,128)(2,1)S(1)}, u32[]{:S(2)}, u32[]{:S(2)}) collective-permute-start(bf16[24,2560]{1,0:T(8,128)(2,1)} %fusion.2), channel_id=1, source_target_pairs={{0,5},{1,6},{2,7},{3,8},{4,9},{5,10},{6,11},{7,12},{8,13},{9,14},{... | collective-permute-start | bytes 368648
  1277.8 244.8 %collective-permute-start.5 = (bf16[24,2560]{1,0:T(8,128)(2,1)}, bf16[24,2560]{1,0:T(8,128)(2,1)S(1)}, u32[]{:S(2)}, u32[]{:S(2)}) collective-permute-start(bf16[24,2560]{1,0:T(8,128)(2,1)} %fusion.2), channel_id=1, source_target_pairs={{0,4},{1,5},{2,6},{3,7},{4,8},{5,9},{6,10},{7,11},{8,12},{9,13},{1... | collective-permute-start | bytes 368648
  1279.3 243.3 %collective-permute-start.4 = (bf16[24,2560]{1,0:T(8,128)(2,1)}, bf16[24,2560]{1,0:T(8,128)(2,1)S(1)}, u32[]{:S(2)}, u32[]{:S(2)}) collective-permute-start(bf16[24,2560]{1,0:T(8,128)(2,1)} %fusion.2), channel_id=1, source_target_pairs={{0,3},{1,4},{2,5},{3,6},{4,7},{5,8},{6,9},{7,10},{8,11},{9,12},{10... | collective-permute-start | bytes 368648
  1280.6 242.0 %collective-permute-start.3 = (bf16[24,2560]{1,0:T(8,128)(2,1)}, bf16[24,2560]{1,0:T(8,128)(2,1)S(1)}, u32[]{:S(2)}, u32[]{:S(2)}) collective-permute-start(bf16[24,2560]{1,0:T(8,128)(2,1)} %fusion.2), channel_id=1, source_target_pairs={{0,2},{1,3},{2,4},{3,5},{4,6},{5,7},{6,8},{7,9},{8,10},{9,11},{10,... | collective-permute-start | bytes 368648
  1283.4 122.2 %collective-permute-start.7 = (bf16[4,2560]{1,0:T(4,128)(2,1)S(1)}, bf16[4,2560]{1,0:T(4,128)(2,1)S(1)}, u32[]{:S(2)}, u32[]{:S(2)}) collective-permute-start(bf16[4,2560]{1,0:T(4,128)(2,1)S(1)} %slice.1262), channel_id=1, source_target_pairs={{0,6},{1,7},{2,8},{3,9},{4,10},{5,11},{6,12},{7,13},{8,14},{9,15},... | collective-permute-start | bytes 61448
  1405.6 117.0 %collective-permute-start.2 = (bf16[24,2560]{1,0:T(8,128)(2,1)S(1)}, bf16[24,2560]{1,0:T(8,128)(2,1)S(1)}, u32[]{:S(2)}, u32[]{:S(2)}) collective-permute-start(bf16[24,2560]{1,0:T(8,128)(2,1)S(1)} %copy-done.77), channel_id=1, source_target_pairs={{0,1},{1,2},{2,3},{3,4},{4,5},{5,6},{6,7},{7,8},{8,9},{9,10},{10,1... | collective-permute-start | bytes 368648
  (331 other events, 992.4 us)
Sparse Core Ops, SparseCore 0:
  11.2 93.1 all-gather.4
  107.0 73.6 all-gather.6
  1186.4 193.5 reduce-scatter.3
where the time goes:
time: 1540 us; the launch traced here: 1530 us
  waiting for transfers between devices  618 us (40%)
  blocking collectives  310 us (20%)
  local copies, waits for them, and re-layouts  199 us (13%)
  starting transfers between devices  180 us (12%)
  other arithmetic  145 us (9%)
  matrix products  59.4 us (4%)
    ppermute x22, waiting for transfers between devices, from_behind(): lax.ppermute(value, axis, [(source, source + steps) for source in range(f...  453 us
    ppermute x22, starting transfers between devices, from_behind(): lax.ppermute(value, axis, [(source, source + steps) for source in range(f...  163 us
    psum x1, blocking collectives, body(): lax.psum((head_term * last_weight, loss_term * last_weight), ('section',...  116 us
    psum x1, blocking collectives, body(): lax.psum(kernel_acc.astype(jnp.bfloat16), 'dp').astype(jnp.float32)  111 us
    another operation x200, local copies, waits for them, and re-layouts, kernel_grad(): return jnp.stack(taps, axis=0)  105 us
    all_gather x1, waiting for transfers between devices, body(): lax.all_gather(weight_in[0], 'dp', axis=0, tiled=True)  91.3 us
    unnamed x1, blocking collectives  84.2 us
    all_gather x1, waiting for transfers between devices, body(): lax.all_gather(weight_out[0], 'dp', axis=0, tiled=True)  72.7 us
  transfers between devices with their start and end apart: 31, of which 24 were waited for; matrix products, arithmetic and copies ran while one was open for 8% of the time, Pallas kernels for 0%

commit v1 on v0

--- a/solution.py
+++ b/solution.py
@@ -170,7 +170,7 @@
     factor = 1.0 / (micro_count * slot_count)
     loss_term, seeds, head_term = head_terms(final, target_maps[0], live, head_weight, factor)
     head_total, loss_total = lax.psum(
-        (head_term * last_weight, loss_term * last_weight), ("section", "dp")
+        lax.psum((head_term * last_weight, loss_term * last_weight), "section"), "dp"
     )
     first_back, second_back = (
         lax.all_gather(weight_in[0], "dp", axis=0, tiled=True),

time: 1540 us -> 1550 us (level)
    psum x1 -> x2, blocking collectives: 116 us -> 112 us  [the longest x1 57.4 us: body(): lax.psum(lax.psum((head_term * last_weight, loss_term * last_weight), 'se...]
where the time goes in v1:
time: 1550 us; the launch traced here: 1530 us
  waiting for transfers between devices  618 us (40%)
  blocking collectives  306 us (20%)
  local copies, waits for them, and re-layouts  199 us (13%)
  starting transfers between devices  181 us (12%)
  other arithmetic  145 us (9%)
  matrix products  59.4 us (4%)
    ppermute x22, waiting for transfers between devices, from_behind(): lax.ppermute(value, axis, [(source, source + steps) for source in range(f...  453 us
    ppermute x22, starting transfers between devices, from_behind(): lax.ppermute(value, axis, [(source, source + steps) for source in range(f...  163 us
    psum x1, blocking collectives, body(): lax.psum(kernel_acc.astype(jnp.bfloat16), 'dp').astype(jnp.float32)  111 us
    another operation x200, local copies, waits for them, and re-layouts, kernel_grad(): return jnp.stack(taps, axis=0)  105 us
    all_gather x1, waiting for transfers between devices, body(): lax.all_gather(weight_in[0], 'dp', axis=0, tiled=True)  91.3 us
    unnamed x1, blocking collectives  83.6 us
    all_gather x1, waiting for transfers between devices, body(): lax.all_gather(weight_out[0], 'dp', axis=0, tiled=True)  72.7 us
    psum x1, blocking collectives, body(): lax.psum(lax.psum((head_term * last_weight, loss_term * last_weight), 'se...  57.4 us
  transfers between devices with their start and end apart: 31, of which 24 were waited for; matrix products, arithmetic and copies ran while one was open for 8% of the time, Pallas kernels for 0%

profile of v1, /device:TPU:1, one launch (start us, length us, event | category | flops | bytes accessed | tf_op | source)
XLA Modules:
  0.0 1530.6 jit_solution(1258487595599113366)
XLA Ops:
  13.1 91.3 %all-gather.5.cloned.1.call-done = bf16[1,640,2560]{2,0,1:T(2,128)(2,1)} async-done(((bf16[1,20,2560]{2,0,1:T(2,128)(2,1)}), bf16[1,640,2560]{2,0,1:T(2,128)(2,1)}) %all-gather.5.cloned.1.call-update) | async-done | bytes 3276816 | tf_op jit(solution)/shard_map/all_gather | solution.py:135
  108.0 72.7 %all-gather.7.cloned.1.call-done = bf16[1,2560,640]{2,1,0:T(8,128)(2,1)} async-done(((bf16[1,80,640]{2,1,0:T(8,128)(2,1)}), bf16[1,2560,640]{2,1,0:T(8,128)(2,1)}) %all-gather.7.cloned.1.call-update) | async-done | bytes 3276816 | tf_op jit(solution)/shard_map/all_gather | solution.py:136
  183.2 210.7 %while.40 = (s32[]{:T(128)}, bf16[2,8,8,640]{3,2,1,0:T(8,128)(2,1)}, bf16[4,2,8,8,640]{4,3,2,1,0:T(8,128)(2,1)}, bf16[4,2,8,8,640]{4,3,2,1,0:T(8,128)(2,1)}, s32...) while((s32[]{:T(128)}, ...), condition=%wide.region_5.6_spmd, body=%wide.region_0.5_spmd.sunk | while | flops 849510528 | bytes 13491009 | solution.py:165
  185.9 7.7 collective-permute-start
  195.4 12.2 collective-permute-done
  210.3 14.7 conditional.5
  231.9 14.7 conditional.5
  256.1 14.7 conditional.5
  280.3 14.7 conditional.5
  304.5 19.2 %collective-permute-start = (bf16[2,8,8,640]{3,2,1,0:T(8,128)(2,1)S(1)}, bf16[2,8,8,640]{3,2,1,0:T(8,128)(2,1)}, u32[]{:S(2)}, u32[]{:S(2)}) collective-permute-start(bf16[2,8,8,640]{3,2,1,0:T(8,128)(2,1)S(1)} %get-tuple-element.1155), channel_id=1, source_target_pairs={{0,32},{32,64},{64,96},{96,128},{128,160},{160,192},{192,224},{1,3... | collective-permute-start | bytes 491528 | tf_op jit(solution)/shard_map/while/body/eval_jaxpr/ppermute | solution.py:14
  338.2 12.7 collective-permute-start
  365.5 16.6 %collective-permute-start = (bf16[2,8,8,640]{3,2,1,0:T(8,128)(2,1)S(1)}, bf16[2,8,8,640]{3,2,1,0:T(8,128)(2,1)}, u32[]{:S(2)}, u32[]{:S(2)}) collective-permute-start(bf16[2,8,8,640]{3,2,1,0:T(8,128)(2,1)S(1)} %get-tuple-element.1155), channel_id=1, source_target_pairs={{0,32},{32,64},{64,96},{96,128},{128,160},{160,192},{192,224},{1,3... | collective-permute-start | bytes 491528 | tf_op jit(solution)/shard_map/while/body/eval_jaxpr/ppermute | solution.py:14
  403.2 778.1 %while.41 = (s32[]{:T(128)}, bf16[2,8,8,640]{3,2,1,0:T(8,128)(2,1)}, f32[49,640]{1,0:T(8,128)S(1)}, f32[640,2560]{1,0:T(8,128)}, f32[2560,640]{1,0:T(8,128)}, /*...) while((s32[]{:T(128)}, ...), condition=%wide.region_63.64_spmd.clone, body=%wide.region_7.63_spmd.clone.sunk | while | flops 2131804288 | bytes 130983528 | solution.py:212
  407.5 14.1 collective-permute-done.1
  435.2 17.3 %collective-permute-done.1 = bf16[2,8,8,640]{3,2,1,0:T(8,128)(2,1)} collective-permute-done((bf16[2,8,8,640]{3,2,1,0:T(8,128)(2,1)}, bf16[2,8,8,640]{3,2,1,0:T(8,128)(2,1)}, u32[]{:S(2)}, u32[]{:S(2)}) %collective-permute-start.1) | collective-permute-done | bytes 163872 | tf_op jit(solution)/shard_map/while/body/eval_jaxpr/ppermute | solution.py:14
  466.1 13.4 collective-permute-done.1
  483.8 359.0 %collective-permute-done.1 = bf16[2,8,8,640]{3,2,1,0:T(8,128)(2,1)} collective-permute-done((bf16[2,8,8,640]{3,2,1,0:T(8,128)(2,1)}, bf16[2,8,8,640]{3,2,1,0:T(8,128)(2,1)}, u32[]{:S(2)}, u32[]{:S(2)}) %collective-permute-start.1) | collective-permute-done | bytes 163872 | tf_op jit(solution)/shard_map/while/body/eval_jaxpr/ppermute | solution.py:14
  844.6 60.5 %conditional.6 = (bf16[2,8,8,640]{3,2,1,0:T(8,128)(2,1)}, f32[49,640]{1,0:T(8,128)S(1)}, f32[640,2560]{1,0:T(8,128)}, f32[2560,640]{1,0:T(8,128)}) conditional(s32[]{:T(128)} %convert_element_type.175, (f32[49,640]{1,0:T(8,128)S(1)}, f32[640,2560]{1,0:T(8,128)}, f32[2560,640]{1,0:T(8,128)}) %tuple.251, (pred[]{:T(512)}, s32[]{:T(128)}, ...), branch_computations={%region_8.8_spmd, %region_9.62_spmd} | conditional | flops 2131148928 | bytes 129667864 | solution.py:206
  884.0 8.0 stack.299
  913.7 60.5 %conditional.6 = (bf16[2,8,8,640]{3,2,1,0:T(8,128)(2,1)}, f32[49,640]{1,0:T(8,128)S(1)}, f32[640,2560]{1,0:T(8,128)}, f32[2560,640]{1,0:T(8,128)}) conditional(s32[]{:T(128)} %convert_element_type.175, (f32[49,640]{1,0:T(8,128)S(1)}, f32[640,2560]{1,0:T(8,128)}, f32[2560,640]{1,0:T(8,128)}) %tuple.251, (pred[]{:T(512)}, s32[]{:T(128)}, ...), branch_computations={%region_8.8_spmd, %region_9.62_spmd} | conditional | flops 2131148928 | bytes 129667864 | solution.py:206
  953.1 8.0 stack.299
  982.8 60.5 %conditional.6 = (bf16[2,8,8,640]{3,2,1,0:T(8,128)(2,1)}, f32[49,640]{1,0:T(8,128)S(1)}, f32[640,2560]{1,0:T(8,128)}, f32[2560,640]{1,0:T(8,128)}) conditional(s32[]{:T(128)} %convert_element_type.175, (f32[49,640]{1,0:T(8,128)S(1)}, f32[640,2560]{1,0:T(8,128)}, f32[2560,640]{1,0:T(8,128)}) %tuple.251, (pred[]{:T(512)}, s32[]{:T(128)}, ...), branch_computations={%region_8.8_spmd, %region_9.62_spmd} | conditional | flops 2131148928 | bytes 129667864 | solution.py:206
  1022.2 8.0 stack.299
  1051.9 60.5 %conditional.6 = (bf16[2,8,8,640]{3,2,1,0:T(8,128)(2,1)}, f32[49,640]{1,0:T(8,128)S(1)}, f32[640,2560]{1,0:T(8,128)}, f32[2560,640]{1,0:T(8,128)}) conditional(s32[]{:T(128)} %convert_element_type.175, (f32[49,640]{1,0:T(8,128)S(1)}, f32[640,2560]{1,0:T(8,128)}, f32[2560,640]{1,0:T(8,128)}) %tuple.251, (pred[]{:T(512)}, s32[]{:T(128)}, ...), branch_computations={%region_8.8_spmd, %region_9.62_spmd} | conditional | flops 2131148928 | bytes 129667864 | solution.py:206
  1091.3 8.0 stack.299
  1101.1 7.2 convolution_add_fusion.1
  1121.6 58.4 %collective-permute-start.1 = (bf16[2,8,8,640]{3,2,1,0:T(8,128)(2,1)}, bf16[2,8,8,640]{3,2,1,0:T(8,128)(2,1)}, u32[]{:S(2)}, u32[]{:S(2)}) collective-permute-start(bf16[2,8,8,640]{3,2,1,0:T(8,128)(2,1)} %get-tuple-element.1053), channel_id=1, source_target_pairs={{32,0},{64,32},{96,64},{128,96},{160,128},{192,160},{224,192},{33,... | collective-permute-start | bytes 491528 | tf_op jit(solution)/shard_map/while/body/eval_jaxpr/ppermute | solution.py:14
  1191.4 83.6 %fusion.2 = bf16[24,2560]{1,0:T(8,128)(2,1)} fusion(bf16[640,2560]{1,0:T(8,128)(2,1)S(1)} %convert_element_type.133), kind=kCustom, calls=%all-reduce-scatter | all-reduce-scatter fusion | flops 1966081 | bytes 3400704
  1283.7 10.3 collective-permute-start.7
  1295.4 110.9 %psum.35 = bf16[1,49,640]{2,0,1:T(2,128)(2,1)S(1)} all-reduce(bf16[1,49,640]{2,0,1:T(2,128)(2,1)S(1)} %broadcast_in_dim.64), channel_id=1, replica_groups=mesh['section'=8,'dp'=32] {'dp'}, use_global_device_ids=true, to_apply=%region_66.67 | all-reduce | flops 31360 | bytes 125440 | tf_op jit(solution)/shard_map/psum | solution.py:223
  1408.3 54.4 %all-reduce.6 = (f32[640]{0:T(1024)S(1)}, f32[]{:T(128)}) all-reduce(f32[640]{0:T(1024)S(1)} %broadcast_multiply_fusion.4, f32[]{:T(128)S(6)} %mul.2377), channel_id=1, replica_groups=mesh['section'=8,'dp'=32] {'section'}, use_global_device_ids=true, to_apply=%region_68.69 | all-reduce | flops 641 | bytes 5128 | tf_op jit(solution)/shard_map/psum | solution.py:173
  1462.7 57.4 %all-reduce.5 = (f32[640]{0:T(1024)}, f32[]{:T(128)}) all-reduce(f32[640]{0:T(1024)S(1)} %get-tuple-element.886, f32[]{:T(128)} %get-tuple-element.887), channel_id=1, replica_groups=mesh['section'=8,'dp'=32] {'dp'}, use_global_device_ids=true, to_apply=%region_69.70 | all-reduce | flops 641 | bytes 5128 | tf_op jit(solution)/shard_map/psum | solution.py:172
  (1169 shorter events, 464.3 us)
Async XLA Ops:
  7.2 97.2 %all-gather.5.cloned.1.call-start = ((), (), s32[]{:S(2)}) async-start(), calls=%async_computation.2 | async-start | bytes 6758400 | tf_op jit(solution)/shard_map/all_gather | solution.py:135
  9.0 171.6 %all-gather.7.cloned.1.call-start = ((), (), s32[]{:S(2)}) async-start(), calls=%async_computation.3 | async-start | bytes 3379200 | tf_op jit(solution)/shard_map/all_gather | solution.py:136
  9.8 1512.7 %reduce-scatter.4.cloned.1.call-start = ((), (), s32[]{:S(2)}) async-start(), calls=%async_computation.1 | async-start | bytes 3379200 | tf_op jit(solution)/shard_map/reduce_scatter | solution.py:219
  183.2 212.0 %copy-start.81 = (s32[1,4,2,8,8]{4,3,2,1,0:T(8,128)S(1)}, s32[1,4,2,8,8]{4,3,2,1,0:T(8,128)}, u32[]{:S(2)}) copy-start(s32[1,4,2,8,8]{4,3,2,1,0:T(8,128)} %param.16) | copy-start | bytes 6148
  185.9 21.6 %collective-permute-start = (bf16[2,8,8,640]{3,2,1,0:T(8,128)(2,1)S(1)}, bf16[2,8,8,640]{3,2,1,0:T(8,128)(2,1)}, u32[]{:S(2)}, u32[]{:S(2)}) collective-permute-start(bf16[2,8,8,640]{3,2,1,0:T(8,128)(2,1)S(1)} %get-tuple-element.1155), channel_id=1, source_target_pairs={{0,32},{32,64},{64,96},{96,128},{128,160},{160,192},{192,224},{1,3... | collective-permute-start | bytes 491528 | tf_op jit(solution)/shard_map/while/body/eval_jaxpr/ppermute | solution.py:14
  225.0 4.2 collective-permute-start
  246.6 6.8 collective-permute-start
  270.8 6.7 collective-permute-start
  295.0 6.7 collective-permute-start
  304.5 21.4 %collective-permute-start = (bf16[2,8,8,640]{3,2,1,0:T(8,128)(2,1)S(1)}, bf16[2,8,8,640]{3,2,1,0:T(8,128)(2,1)}, u32[]{:S(2)}, u32[]{:S(2)}) collective-permute-start(bf16[2,8,8,640]{3,2,1,0:T(8,128)(2,1)S(1)} %get-tuple-element.1155), channel_id=1, source_target_pairs={{0,32},{32,64},{64,96},{96,128},{128,160},{160,192},{192,224},{1,3... | collective-permute-start | bytes 491528 | tf_op jit(solution)/shard_map/while/body/eval_jaxpr/ppermute | solution.py:14
  328.7 6.7 collective-permute-start
  338.2 14.9 collective-permute-start
  355.9 6.7 collective-permute-start
  365.5 18.8 %collective-permute-start = (bf16[2,8,8,640]{3,2,1,0:T(8,128)(2,1)S(1)}, bf16[2,8,8,640]{3,2,1,0:T(8,128)(2,1)}, u32[]{:S(2)}, u32[]{:S(2)}) collective-permute-start(bf16[2,8,8,640]{3,2,1,0:T(8,128)(2,1)S(1)} %get-tuple-element.1155), channel_id=1, source_target_pairs={{0,32},{32,64},{64,96},{96,128},{128,160},{160,192},{192,224},{1,3... | collective-permute-start | bytes 491528 | tf_op jit(solution)/shard_map/while/body/eval_jaxpr/ppermute | solution.py:14
  387.1 6.7 collective-permute-start
  405.6 16.0 %collective-permute-start.1 = (bf16[2,8,8,640]{3,2,1,0:T(8,128)(2,1)}, bf16[2,8,8,640]{3,2,1,0:T(8,128)(2,1)}, u32[]{:S(2)}, u32[]{:S(2)}) collective-permute-start(bf16[2,8,8,640]{3,2,1,0:T(8,128)(2,1)} %get-tuple-element.1053), channel_id=1, source_target_pairs={{32,0},{64,32},{96,64},{128,96},{160,128},{192,160},{224,192},{33,... | collective-permute-start | bytes 491528 | tf_op jit(solution)/shard_map/while/body/eval_jaxpr/ppermute | solution.py:14
  423.9 6.9 collective-permute-start.1
  433.3 19.2 %collective-permute-start.1 = (bf16[2,8,8,640]{3,2,1,0:T(8,128)(2,1)}, bf16[2,8,8,640]{3,2,1,0:T(8,128)(2,1)}, u32[]{:S(2)}, u32[]{:S(2)}) collective-permute-start(bf16[2,8,8,640]{3,2,1,0:T(8,128)(2,1)} %get-tuple-element.1053), channel_id=1, source_target_pairs={{32,0},{64,32},{96,64},{128,96},{160,128},{192,160},{224,192},{33,... | collective-permute-start | bytes 491528 | tf_op jit(solution)/shard_map/while/body/eval_jaxpr/ppermute | solution.py:14
  454.9 6.9 collective-permute-start.1
  464.2 15.3 %collective-permute-start.1 = (bf16[2,8,8,640]{3,2,1,0:T(8,128)(2,1)}, bf16[2,8,8,640]{3,2,1,0:T(8,128)(2,1)}, u32[]{:S(2)}, u32[]{:S(2)}) collective-permute-start(bf16[2,8,8,640]{3,2,1,0:T(8,128)(2,1)} %get-tuple-element.1053), channel_id=1, source_target_pairs={{32,0},{64,32},{96,64},{128,96},{160,128},{192,160},{224,192},{33,... | collective-permute-start | bytes 491528 | tf_op jit(solution)/shard_map/while/body/eval_jaxpr/ppermute | solution.py:14
  481.9 360.9 %collective-permute-start.1 = (bf16[2,8,8,640]{3,2,1,0:T(8,128)(2,1)}, bf16[2,8,8,640]{3,2,1,0:T(8,128)(2,1)}, u32[]{:S(2)}, u32[]{:S(2)}) collective-permute-start(bf16[2,8,8,640]{3,2,1,0:T(8,128)(2,1)} %get-tuple-element.1053), channel_id=1, source_target_pairs={{32,0},{64,32},{96,64},{128,96},{160,128},{192,160},{224,192},{33,... | collective-permute-start | bytes 491528 | tf_op jit(solution)/shard_map/while/body/eval_jaxpr/ppermute | solution.py:14
  905.0 6.9 collective-permute-start.1
  974.1 6.9 collective-permute-start.1
  1043.2 6.9 collective-permute-start.1
  1112.3 6.9 collective-permute-start.1
  1121.6 59.7 %collective-permute-start.1 = (bf16[2,8,8,640]{3,2,1,0:T(8,128)(2,1)}, bf16[2,8,8,640]{3,2,1,0:T(8,128)(2,1)}, u32[]{:S(2)}, u32[]{:S(2)}) collective-permute-start(bf16[2,8,8,640]{3,2,1,0:T(8,128)(2,1)} %get-tuple-element.1053), channel_id=1, source_target_pairs={{32,0},{64,32},{96,64},{128,96},{160,128},{192,160},{224,192},{33,... | collective-permute-start | bytes 491528 | tf_op jit(solution)/shard_map/while/body/eval_jaxpr/ppermute | solution.py:14
  1275.8 244.3 %collective-permute-start.6 = (bf16[24,2560]{1,0:T(8,128)(2,1)}, bf16[24,2560]{1,0:T(8,128)(2,1)S(1)}, u32[]{:S(2)}, u32[]{:S(2)}) collective-permute-start(bf16[24,2560]{1,0:T(8,128)(2,1)} %fusion.2), channel_id=1, source_target_pairs={{0,5},{1,6},{2,7},{3,8},{4,9},{5,10},{6,11},{7,12},{8,13},{9,14},{... | collective-permute-start | bytes 368648
  1277.2 243.0 %collective-permute-start.5 = (bf16[24,2560]{1,0:T(8,128)(2,1)}, bf16[24,2560]{1,0:T(8,128)(2,1)S(1)}, u32[]{:S(2)}, u32[]{:S(2)}) collective-permute-start(bf16[24,2560]{1,0:T(8,128)(2,1)} %fusion.2), channel_id=1, source_target_pairs={{0,4},{1,5},{2,6},{3,7},{4,8},{5,9},{6,10},{7,11},{8,12},{9,13},{1... | collective-permute-start | bytes 368648
  1278.7 241.5 %collective-permute-start.4 = (bf16[24,2560]{1,0:T(8,128)(2,1)}, bf16[24,2560]{1,0:T(8,128)(2,1)S(1)}, u32[]{:S(2)}, u32[]{:S(2)}) collective-permute-start(bf16[24,2560]{1,0:T(8,128)(2,1)} %fusion.2), channel_id=1, source_target_pairs={{0,3},{1,4},{2,5},{3,6},{4,7},{5,8},{6,9},{7,10},{8,11},{9,12},{10... | collective-permute-start | bytes 368648
  1280.0 240.2 %collective-permute-start.3 = (bf16[24,2560]{1,0:T(8,128)(2,1)}, bf16[24,2560]{1,0:T(8,128)(2,1)S(1)}, u32[]{:S(2)}, u32[]{:S(2)}) collective-permute-start(bf16[24,2560]{1,0:T(8,128)(2,1)} %fusion.2), channel_id=1, source_target_pairs={{0,2},{1,3},{2,4},{3,5},{4,6},{5,7},{6,8},{7,9},{8,10},{9,11},{10,... | collective-permute-start | bytes 368648
  1283.7 123.4 %collective-permute-start.7 = (bf16[4,2560]{1,0:T(4,128)(2,1)S(1)}, bf16[4,2560]{1,0:T(4,128)(2,1)S(1)}, u32[]{:S(2)}, u32[]{:S(2)}) collective-permute-start(bf16[4,2560]{1,0:T(4,128)(2,1)S(1)} %slice.1262), channel_id=1, source_target_pairs={{0,6},{1,7},{2,8},{3,9},{4,10},{5,11},{6,12},{7,13},{8,14},{9,15},... | collective-permute-start | bytes 61448
  1407.0 113.1 %collective-permute-start.2 = (bf16[24,2560]{1,0:T(8,128)(2,1)S(1)}, bf16[24,2560]{1,0:T(8,128)(2,1)S(1)}, u32[]{:S(2)}, u32[]{:S(2)}) collective-permute-start(bf16[24,2560]{1,0:T(8,128)(2,1)S(1)} %copy-done.77), channel_id=1, source_target_pairs={{0,1},{1,2},{2,3},{3,4},{4,5},{5,6},{6,7},{7,8},{8,9},{9,10},{10,1... | collective-permute-start | bytes 368648
  (331 other events, 994.4 us)
Sparse Core Ops, SparseCore 0:
  11.2 93.1 all-gather.4
  107.0 73.6 all-gather.6
  1186.4 195.3 reduce-scatter.3
